TPU v7x, 32 devices: a whole 2x2x4 slice. The times are simulated.
32 devices in a mesh: lon: 2 (over x), lat: 16 (over z, y, core).
Axes of the slice: x: 2, y: 2, z: 4, core: 2. Of those that a mesh axis runs over, the one named last changes fastest.
Arguments:
- state: bfloat16 [1, 128, 256, 128], P(None, 'lat', 'lon'), may hold values from -6 to 6
- mix_weight: bfloat16 [128, 2, 128, 128], P('lat'), may hold values from -0.375 to 0.375
- skip_weight: bfloat16 [128, 128], replicated, may hold values from -0.5 to 0.5
Outputs:
- output: bfloat16 [1, 128, 256, 128], P(None, 'lat', 'lon')
All inputs are finite; a program needn't handle non-finite values.
Results may differ from a plain program's by a relative error of at most 0.008.
Values may be sent and summed in bfloat16 or wider, within the bound.
A program may use at most 64 MiB of HBM per device.

v0:
```python
import math

import jax
import jax.numpy as jnp
from jax import lax
from jax.sharding import PartitionSpec as P

rescale_limit = 1e18
log_rescale = 18.0 * math.log(10.0)


def lat_geometry(lat_count):
    positions = jnp.arange(lat_count, dtype=jnp.float32)
    colatitude = jnp.pi * (positions + 0.5) / lat_count
    return (jnp.cos(colatitude), jnp.sin(colatitude))


def fourier_tables(lon_count, mode_count):
    lon_index = jnp.arange(lon_count, dtype=jnp.int32)[:, None]
    mode_index = jnp.arange(mode_count, dtype=jnp.int32)[None, :]
    angles = (lon_index * mode_index % lon_count).astype(jnp.float32) * (2.0 * math.pi / lon_count)
    norming = 1.0 / math.sqrt(lon_count)
    paired = jnp.stack([jnp.cos(angles), -jnp.sin(angles)], axis=2) * norming
    weight = jnp.where(mode_index == 0, 1.0, 2.0)[:, :, None]
    forward = paired.reshape(lon_count, 2 * mode_count).astype(jnp.bfloat16)
    backward = (paired * weight).reshape(lon_count, 2 * mode_count).astype(jnp.bfloat16)
    return (forward, backward)


def legendre_tables(mode_ids, lat_count, degrees):
    cosine, sine_values = lat_geometry(lat_count)
    count = mode_ids.shape[0]
    layout = (1, lat_count // 128, 128)
    orders = mode_ids.astype(jnp.float32)[:, None]
    counter = jnp.arange(1, degrees + 1, dtype=jnp.float32)
    halves = 0.5 * jnp.log((2.0 * counter + 1.0) / (2.0 * counter))
    summed = jnp.sum(
        jnp.where(counter[None, :] <= orders, halves[None, :], jnp.float32(0.0)),
        axis=1,
        keepdims=True,
    )
    log_start = 0.5 * jnp.log(jnp.float32(0.5)) + summed + orders * jnp.log(sine_values)[None, :]
    log_start = log_start.reshape((count,) + layout[1:])
    orders = orders.reshape(count, 1, 1)
    cosine = cosine.reshape(layout)
    sine_values = sine_values.reshape(layout)
    analysis_scale = math.pi / math.sqrt(lat_count)
    synthesis_scale = 1.0 / math.sqrt(degrees)
    zeros = jnp.zeros((count,) + layout[1:], jnp.float32)

    def advance(carry, level_index):
        previous, earlier, exponent = carry
        level = level_index.astype(jnp.float32)
        ratio_a = jnp.sqrt(
            jnp.maximum(4.0 * level * level - 1.0, 0.0)
            / jnp.maximum(level * level - orders * orders, 1.0)
        )
        below = level - 1.0
        ratio_b = jnp.sqrt(
            jnp.maximum(below * below - orders * orders, 0.0)
            / jnp.maximum(4.0 * below * below - 1.0, 1.0)
        )
        raised = ratio_a * (cosine * previous - ratio_b * earlier)
        at_start = level == orders
        current = jnp.where(at_start, 1.0, jnp.where(level > orders, raised, 0.0))
        exponent = jnp.where(at_start, log_start, exponent)
        oversize = jnp.abs(current) > rescale_limit
        factor = jnp.where(oversize, 1.0 / rescale_limit, 1.0)
        earlier = previous * factor
        previous = current * factor
        exponent = exponent + jnp.where(oversize, log_rescale, 0.0)
        value = previous * jnp.exp(exponent)
        analysis_row = (value * analysis_scale * sine_values).astype(jnp.bfloat16)
        synthesis_row = (value * synthesis_scale).astype(jnp.bfloat16)
        return ((previous, earlier, exponent), (analysis_row, synthesis_row))

    levels = jnp.arange(degrees, dtype=jnp.int32)
    outputs = lax.scan(advance, (zeros, zeros, zeros), levels, unroll=32)[1]
    analysis = outputs[0].reshape(degrees, count, lat_count)
    synthesis = outputs[1].reshape(degrees, count, lat_count)
    return (analysis, synthesis)


def mixing_blocks(mix_weight):
    real_part = mix_weight[:, 0]
    imag_part = mix_weight[:, 1]
    upper = jnp.concatenate([real_part, imag_part], axis=2)
    lower = jnp.concatenate([-imag_part, real_part], axis=2)
    return jnp.concatenate([upper, lower], axis=1)


def shards(state, mix_weight, skip_weight):
    samples, lat_dev, lon_dev, channels = state.shape
    lon_groups = lax.axis_size("lon")
    lat_groups = lax.axis_size("lat")
    lon_count = lon_dev * lon_groups
    lat_count = lat_dev * lat_groups
    mode_count = lon_count // 2
    lon_modes = mode_count // lon_groups
    own_modes = lon_modes // lat_groups
    forward, backward = fourier_tables(lon_count, mode_count)
    first_mode = lax.axis_index("lon") * lon_modes + lax.axis_index("lat") * own_modes
    mode_ids = first_mode + jnp.arange(own_modes, dtype=jnp.int32)
    analysis, synthesis = legendre_tables(mode_ids, lat_count, mode_count)
    block_weight = mixing_blocks(mix_weight)
    received = lax.all_to_all(state, "lon", split_axis=1, concat_axis=2, tiled=True)
    items = received.shape[0]
    row_count = received.shape[1]
    spectra = jnp.einsum(
        "sjkc,kq->sjqc", received, forward, preferred_element_type=jnp.float32
    ).astype(jnp.bfloat16)
    spectra = spectra.reshape(items, row_count, lon_groups, 2 * lon_modes, channels)
    spectra = lax.all_to_all(spectra, "lon", split_axis=2, concat_axis=1, tiled=True)
    spectrum = spectra.reshape(items, lat_dev, 2 * lon_modes, channels)
    received = lax.all_to_all(spectrum, "lat", split_axis=2, concat_axis=1, tiled=True)
    items = received.shape[0]
    pieces = received.reshape(items, lat_count, own_modes, 2, channels)
    coeffs = jnp.einsum(
        "lij,sjirc->slirc", analysis, pieces, preferred_element_type=jnp.float32
    ).astype(jnp.bfloat16)
    coeffs = coeffs.reshape(items, mode_count, 2 * own_modes, channels)
    coefficients = lax.all_to_all(coeffs, "lat", split_axis=1, concat_axis=2, tiled=True)
    deg_dev = coefficients.shape[1]
    paired = coefficients.reshape(samples, deg_dev, lon_modes, 2 * channels)
    mixed = jnp.einsum(
        "slix,lxy->sliy", paired, block_weight, preferred_element_type=jnp.float32
    ).astype(jnp.bfloat16)
    mixed = mixed.reshape(samples, deg_dev, 2 * lon_modes, channels)
    received = lax.all_to_all(mixed, "lat", split_axis=2, concat_axis=1, tiled=True)
    items = received.shape[0]
    pieces = received.reshape(items, mode_count, own_modes, 2 * channels)
    gridded = jnp.einsum(
        "lij,sliy->sjiy", synthesis, pieces, preferred_element_type=jnp.float32
    ).astype(jnp.bfloat16)
    gridded = gridded.reshape(items, lat_count, 2 * own_modes, channels)
    grid_modes = lax.all_to_all(gridded, "lat", split_axis=1, concat_axis=2, tiled=True)
    grid_modes = grid_modes.reshape(samples, lat_dev, 1, 2 * lon_modes, channels)
    received = lax.all_to_all(grid_modes, "lon", split_axis=1, concat_axis=2, tiled=True)
    items = received.shape[0]
    row_count = received.shape[1]
    spectra = received.reshape(items, row_count, 2 * mode_count, channels)
    values = jnp.einsum(
        "sjqc,kq->sjkc", spectra, backward, preferred_element_type=jnp.float32
    ).astype(jnp.bfloat16)
    spectral = lax.all_to_all(values, "lon", split_axis=2, concat_axis=1, tiled=True)
    local_term = jnp.einsum("sjkc,cd->sjkd", state, skip_weight, preferred_element_type=jnp.float32)
    return jax.nn.gelu(spectral.astype(jnp.float32) + local_term).astype(jnp.bfloat16)


def solution(mesh):
    placed = (P(None, "lat", "lon", None), P("lat", None, None, None), P())
    return jax.shard_map(
        shards, mesh=mesh, in_specs=placed, out_specs=P(None, "lat", "lon", None), check_vma=False
    )
```

profile of v0, /device:TPU:0, one launch (start us, length us, event | category | flops | bytes accessed | tf_op | source)
XLA Modules:
  0.0 206.9 jit_solution(11996657977514319588)
XLA Ops:
  0.0 4.4 %all-to-all-start = ((bf16[1,8,128,128]{3,2,0,1:T(8,128)(2,1)}), bf16[1,8,128,128]{3,2,0,1:T(8,128)(2,1)S(1)}, u32[]{:S(2)}, u32[]{:S(2)}) async-start(bf16[1,8,128,128]{3,2,0,1:T(8,128)(2,1)} %bitcast.1187), calls=%async_computation | async-start | bytes 524288 | tf_op jit(solution)/shard_map/all_to_all | solution.py:106
  4.4 0.5 sine_negate_fusion
  5.4 4.8 %all-to-all-done = bf16[1,8,128,128]{3,2,0,1:T(8,128)(2,1)S(1)} async-done(((bf16[1,8,128,128]{3,2,0,1:T(8,128)(2,1)}), bf16[1,8,128,128]{3,2,0,1:T(8,128)(2,1)S(1)}, u32[]{:S(2)}, u32[]{:S(2)}) %all-to-all-start) | async-done | bytes 262176 | tf_op jit(solution)/shard_map/all_to_all | solution.py:106
  10.5 0.7 copy.342
  11.2 3.4 %all-to-all-start.1 = ((bf16[1,4,2,128,128]{4,3,1,0,2:T(8,128)(2,1)}), bf16[1,4,2,128,128]{4,3,1,0,2:T(8,128)(2,1)S(1)}, u32[]{:S(2)}, u32[]{:S(2)}) async-start(bf16[1,4,2,128,128]{4,3,1,0,2:T(8,128)(2,1)} %copy.342), calls=%async_computation.1 | async-start | bytes 524288 | tf_op jit(solution)/shard_map/all_to_all | solution.py:113
  14.8 5.1 %all-to-all-done.1 = bf16[1,4,2,128,128]{4,3,1,0,2:T(8,128)(2,1)S(1)} async-done(((bf16[1,4,2,128,128]{4,3,1,0,2:T(8,128)(2,1)}), bf16[1,4,2,128,128]{4,3,1,0,2:T(8,128)(2,1)S(1)}, u32[]{:S(2)}, u32[]{:S(2)}) %all-to-all-start.1) | async-done | bytes 262176 | tf_op jit(solution)/shard_map/all_to_all | solution.py:113
  19.8 0.9 copy.343
  20.7 6.2 %all-to-all-start.2 = ((bf16[1,8,128,128]{3,1,0,2:T(8,128)(2,1)}), bf16[1,8,128,128]{3,1,0,2:T(8,128)(2,1)S(1)}, u32[]{:S(2)}, u32[]{:S(2)}) async-start(bf16[1,8,128,128]{3,1,0,2:T(8,128)(2,1)} %copy.343), calls=%async_computation.2 | async-start | bytes 524288 | tf_op jit(solution)/shard_map/all_to_all | solution.py:115
  26.9 115.9 %while.25 = (s32[]{:T(128)}, f32[4,1,128]{2,0,1:T(4,128)S(1)}, f32[4,1,128]{2,0,1:T(4,128)S(1)}, f32[4,1,128]{2,0,1:T(4,128)S(1)}, bf16[4,32,4,1,128]{4,2,1,3,0:...) while((s32[]{:T(128)}, f32[4,1,128]{2,0,1:T(4,128)S(1)}, ...), condition=%wide.region_2.3_spmd.clone.clone.clone.clone, body=%wide.region_1.2_spmd.clone.clone.clone.clone.sunk | while | flops 619265 | bytes 824448 | solution.py:78
  27.0 0.7 fusion.393
  36.9 0.7 fusion.392
  56.0 0.7 fusion.393
  65.9 0.7 fusion.392
  85.0 0.7 fusion.393
  94.9 0.7 fusion.392
  113.9 0.7 fusion.393
  123.8 0.7 fusion.392
  143.0 0.3 convolution_convert_fusion.3
  143.3 0.9 copy.348
  144.2 6.0 %all-to-all-start.3 = ((bf16[1,128,8,128]{3,2,0,1:T(8,128)(2,1)}), bf16[1,128,8,128]{3,2,0,1:T(8,128)(2,1)S(1)}, u32[]{:S(2)}, u32[]{:S(2)}) async-start(bf16[1,128,8,128]{3,2,0,1:T(8,128)(2,1)} %copy.348), calls=%async_computation.3 | async-start | bytes 524288 | tf_op jit(solution)/shard_map/all_to_all | solution.py:122
  150.3 9.9 %all-to-all-done.3 = bf16[1,128,8,128]{3,2,0,1:T(8,128)(2,1)S(1)} async-done(((bf16[1,128,8,128]{3,2,0,1:T(8,128)(2,1)}), bf16[1,128,8,128]{3,2,0,1:T(8,128)(2,1)S(1)}, u32[]{:S(2)}, u32[]{:S(2)}) %all-to-all-start.3) | async-done | bytes 262176 | tf_op jit(solution)/shard_map/all_to_all | solution.py:122
  160.4 0.3 fusion.298
  160.9 12.7 %all_to_all.114 = bf16[1,8,128,128]{3,1,0,2:T(8,128)(2,1)S(1)} all-to-all(bf16[1,8,128,128]{3,1,0,2:T(8,128)(2,1)S(1)} %copy.350), channel_id=1, replica_groups=mesh['lon'=2,'lat'=16] {'lat'}, dimensions={2} | all-to-all | bytes 524288 | tf_op jit(solution)/shard_map/all_to_all | solution.py:129
  173.9 0.3 convolution_convert_fusion.2
  174.4 12.7 %all_to_all.115 = bf16[1,128,8,128]{3,2,0,1:T(8,128)(2,1)S(1)} all-to-all(bf16[1,128,8,128]{3,2,0,1:T(8,128)(2,1)S(1)} %copy.355), channel_id=1, replica_groups=mesh['lon'=2,'lat'=16] {'lat'}, dimensions={1} | all-to-all | bytes 524288 | tf_op jit(solution)/shard_map/all_to_all | solution.py:136
  187.1 0.8 copy.379
  187.8 3.4 %all-to-all-start.6 = ((bf16[1,8,1,128,128]{4,3,2,0,1:T(8,128)(2,1)}), bf16[1,8,1,128,128]{4,3,2,0,1:T(8,128)(2,1)S(1)}, u32[]{:S(2)}, u32[]{:S(2)}) async-start(bf16[1,8,1,128,128]{4,3,2,0,1:T(8,128)(2,1)} %bitcast.715), calls=%async_computation.6 | async-start | bytes 524288 | tf_op jit(solution)/shard_map/all_to_all | solution.py:138
  191.5 5.3 %all-to-all-done.6 = bf16[1,8,1,128,128]{4,3,2,0,1:T(8,128)(2,1)S(1)} async-done(((bf16[1,8,1,128,128]{4,3,2,0,1:T(8,128)(2,1)}), bf16[1,8,1,128,128]{4,3,2,0,1:T(8,128)(2,1)S(1)}, u32[]{:S(2)}, u32[]{:S(2)}) %all-to-all-start.6) | async-done | bytes 262176 | tf_op jit(solution)/shard_map/all_to_all | solution.py:138
  196.8 0.3 fusion.297
  197.3 7.6 %all_to_all.116 = bf16[1,4,256,128]{3,1,0,2:T(4,128)(2,1)S(1)} all-to-all(bf16[1,4,256,128]{3,1,0,2:T(4,128)(2,1)S(1)} %copy.360), channel_id=1, replica_groups=mesh['lon'=2,'lat'=16] {'lon'}, dimensions={2} | all-to-all | bytes 524288 | tf_op jit(solution)/shard_map/all_to_all | solution.py:145
  204.9 0.9 copy-done.2
  205.8 1.1 fusion.314
  (828 shorter events, 28.4 us)
Async XLA Ops:
  0.0 204.9 %copy-start = (bf16[128,128]{1,0:T(8,128)(2,1)S(1)}, bf16[128,128]{1,0:T(8,128)(2,1)}, u32[]{:S(2)}) copy-start(bf16[128,128]{1,0:T(8,128)(2,1)} %param.7) | copy-start | bytes 98308
  0.0 10.2 %all-to-all-start = ((bf16[1,8,128,128]{3,2,0,1:T(8,128)(2,1)}), bf16[1,8,128,128]{3,2,0,1:T(8,128)(2,1)S(1)}, u32[]{:S(2)}, u32[]{:S(2)}) async-start(bf16[1,8,128,128]{3,2,0,1:T(8,128)(2,1)} %bitcast.1187), calls=%async_computation | async-start | bytes 524288 | tf_op jit(solution)/shard_map/all_to_all | solution.py:106
  11.2 8.6 %all-to-all-start.1 = ((bf16[1,4,2,128,128]{4,3,1,0,2:T(8,128)(2,1)}), bf16[1,4,2,128,128]{4,3,1,0,2:T(8,128)(2,1)S(1)}, u32[]{:S(2)}, u32[]{:S(2)}) async-start(bf16[1,4,2,128,128]{4,3,1,0,2:T(8,128)(2,1)} %copy.342), calls=%async_computation.1 | async-start | bytes 524288 | tf_op jit(solution)/shard_map/all_to_all | solution.py:113
  20.7 122.1 %all-to-all-start.2 = ((bf16[1,8,128,128]{3,1,0,2:T(8,128)(2,1)}), bf16[1,8,128,128]{3,1,0,2:T(8,128)(2,1)S(1)}, u32[]{:S(2)}, u32[]{:S(2)}) async-start(bf16[1,8,128,128]{3,1,0,2:T(8,128)(2,1)} %copy.343), calls=%async_computation.2 | async-start | bytes 524288 | tf_op jit(solution)/shard_map/all_to_all | solution.py:115
  143.3 6.9 %copy-start.1 = (bf16[8,2,128,128]{3,2,1,0:T(8,128)(2,1)S(1)}, bf16[8,2,128,128]{3,2,1,0:T(8,128)(2,1)}, u32[]{:S(2)}) copy-start(bf16[8,2,128,128]{3,2,1,0:T(8,128)(2,1)} %param.6) | copy-start | bytes 1572868
  144.2 16.0 %all-to-all-start.3 = ((bf16[1,128,8,128]{3,2,0,1:T(8,128)(2,1)}), bf16[1,128,8,128]{3,2,0,1:T(8,128)(2,1)S(1)}, u32[]{:S(2)}, u32[]{:S(2)}) async-start(bf16[1,128,8,128]{3,2,0,1:T(8,128)(2,1)} %copy.348), calls=%async_computation.3 | async-start | bytes 524288 | tf_op jit(solution)/shard_map/all_to_all | solution.py:122
  187.8 9.0 %all-to-all-start.6 = ((bf16[1,8,1,128,128]{4,3,2,0,1:T(8,128)(2,1)}), bf16[1,8,1,128,128]{4,3,2,0,1:T(8,128)(2,1)S(1)}, u32[]{:S(2)}, u32[]{:S(2)}) async-start(bf16[1,8,1,128,128]{4,3,2,0,1:T(8,128)(2,1)} %bitcast.715), calls=%async_computation.6 | async-start | bytes 524288 | tf_op jit(solution)/shard_map/all_to_all | solution.py:138
  204.9 1.0 copy-start.2
where the time goes:
time: 209 us; the launch traced here: 207 us
  loops' own time  84.2 us (40%)
  blocking collectives  32.9 us (16%)
  other arithmetic  26.6 us (13%)
  waiting for transfers between devices  25.1 us (12%)
  starting transfers between devices  23.4 us (11%)
  local copies, waits for them, and re-layouts  11.8 us (6%)
  matrix products  2.38 us (1%)
    another operation x1, loops' own time, legendre_tables(): outputs = lax.scan(advance, (zeros, zeros, zeros), levels, unroll=32)[1]  84.2 us
    while x248, other arithmetic  18 us
    all_to_all x1, blocking collectives, shards(): lax.all_to_all(mixed, 'lat', split_axis=2, concat_axis=1, tiled=True)  12.7 us
    all_to_all x1, blocking collectives, shards(): lax.all_to_all(gridded, 'lat', split_axis=1, concat_axis=2, tiled=True)  12.7 us
    all_to_all x1, waiting for transfers between devices, shards(): lax.all_to_all(coeffs, 'lat', split_axis=1, concat_axis=2, tiled=True)  9.91 us
    all_to_all x1, blocking collectives, shards(): lax.all_to_all(values, 'lon', split_axis=2, concat_axis=1, tiled=True)  7.56 us
    all_to_all x1, starting transfers between devices, shards(): lax.all_to_all(spectrum, 'lat', split_axis=2, concat_axis=1, tiled=True)  6.19 us
    all_to_all x1, starting transfers between devices, shards(): lax.all_to_all(coeffs, 'lat', split_axis=1, concat_axis=2, tiled=True)  6 us
  transfers between devices with their start and end apart: 5, of which 4 were waited for; matrix products, arithmetic and copies ran while one was open for 16% of the time, Pallas kernels for 0%

commit v1 on v0

v1 whole, which is shorter than its diff:
```python
import functools
import math

import jax
import jax.numpy as jnp
from jax import lax
from jax.experimental import pallas as pl
from jax.experimental.pallas import tpu as pltpu
from jax.sharding import PartitionSpec as P

MESH = pl.DeviceIdType.MESH
rescale_limit = 1e18
log_rescale = 18.0 * math.log(10.0)
F32 = jnp.float32
BF16 = jnp.bfloat16


def modulo(value, size):
    return value & (size - 1) if size & (size - 1) == 0 else lax.rem(value, size)


def fourier_values(mode_index, part, lon_index, lon_count):
    phase = modulo(lon_index * mode_index + part * (lon_count // 4), lon_count)
    return jnp.cos(phase.astype(F32) * (2.0 * math.pi / lon_count)) * (1.0 / math.sqrt(lon_count))


def build_forward(ft, lon_count, block):
    rows, columns = ft.shape

    def fill(step, carry):
        start = pl.multiple_of(step * block, block)
        q = lax.broadcasted_iota(jnp.int32, (block, columns), 0) + start
        k = lax.broadcasted_iota(jnp.int32, (block, columns), 1)
        ft[pl.ds(start, block), :] = fourier_values(q >> 1, q & 1, k, lon_count).astype(BF16)
        return carry

    lax.fori_loop(0, rows // block, fill, 0)


def build_backward(bt, lon_count, block):
    rows, columns = bt.shape

    def fill(step, carry):
        start = pl.multiple_of(step * block, block)
        k = lax.broadcasted_iota(jnp.int32, (block, columns), 0) + start
        q = lax.broadcasted_iota(jnp.int32, (block, columns), 1)
        weight = jnp.where(q < 2, 1.0, 2.0)
        bt[pl.ds(start, block), :] = (fourier_values(q >> 1, q & 1, k, lon_count) * weight).astype(BF16)
        return carry

    lax.fori_loop(0, rows // block, fill, 0)


def build_legendre(lg, an, syt, first_mode):
    own, degrees, lat_count = lg.shape
    shape = (own, lat_count)
    position = lax.broadcasted_iota(jnp.int32, (1, lat_count), 1).astype(F32)
    colatitude = math.pi * (position + 0.5) / lat_count
    cosine = jnp.cos(colatitude)
    sine = jnp.sin(colatitude)
    orders = (lax.broadcasted_iota(jnp.int32, shape, 0) + first_mode).astype(F32)
    counter = (lax.broadcasted_iota(jnp.int32, (own, degrees), 1) + 1).astype(F32)
    own_order = (lax.broadcasted_iota(jnp.int32, (own, degrees), 0) + first_mode).astype(F32)
    halves = 0.5 * jnp.log((2.0 * counter + 1.0) / (2.0 * counter))
    summed = jnp.sum(jnp.where(counter <= own_order, halves, 0.0), axis=1, keepdims=True)
    log_start = 0.5 * math.log(0.5) + summed + orders * jnp.log(sine)
    squares = orders * orders
    wide_cosine = jnp.broadcast_to(cosine, shape)
    unroll = 8

    def advance(step, carry):
        previous, earlier, exponent = carry
        for offset in range(unroll):
            index = step * unroll + offset
            level = jnp.full(shape, index, jnp.int32).astype(F32)
            ratio_a = jnp.sqrt(
                jnp.maximum(4.0 * level * level - 1.0, 0.0) / jnp.maximum(level * level - squares, 1.0)
            )
            below = level - 1.0
            ratio_b = jnp.sqrt(
                jnp.maximum(below * below - squares, 0.0)
                / jnp.maximum(4.0 * below * below - 1.0, 1.0)
            )
            raised = ratio_a * (wide_cosine * previous - ratio_b * earlier)
            at_start = level == orders
            current = jnp.where(at_start, 1.0, jnp.where(level > orders, raised, 0.0))
            exponent = jnp.where(at_start, log_start, exponent)
            oversize = jnp.abs(current) > rescale_limit
            factor = jnp.where(oversize, 1.0 / rescale_limit, 1.0)
            earlier = previous * factor
            previous = current * factor
            exponent = exponent + jnp.where(oversize, log_rescale, 0.0)
            value = previous * jnp.exp(exponent)
            for i in range(own):
                lg[i, pl.ds(index, 1), :] = value[i : i + 1]
        return previous, earlier, exponent

    zeros = jnp.zeros(shape, F32)
    lax.fori_loop(0, degrees // unroll, advance, (zeros, zeros, zeros))
    for i in range(own):
        value = lg[i]
        an[i] = (value * (math.pi / math.sqrt(lat_count)) * sine).astype(BF16)
        syt[i] = jnp.transpose(value * (1.0 / math.sqrt(degrees))).astype(BF16)


def gelu(v):
    return 0.5 * v * (1.0 + jnp.tanh(math.sqrt(2.0 / math.pi) * (v + 0.044715 * v * v * v)))


def kernel(
    L, G, state, mix, skip, out,
    st, mx, sk, ra, sb, rb, sc, rc, sd, rd, se, re, sf, rf,
    ft, bt, lg, an, syt, wb, scr, scm, local,
    sem_in, sem_own, sem_a, sem_ra, sem_s, sem_r, sem_f, sem_rf,
):
    N = L * G
    J, KD, C = st.shape
    R = J // L
    D = mx.shape[0]
    K = KD * L
    own = lg.shape[0]
    Q = 2 * own * N
    LAT = J * G
    DEG = D * G
    a = lax.axis_index("lon")
    g = lax.axis_index("lat")
    n = g * L + a

    def place(p):
        return (lax.rem(p, L), p // L)

    loads = [
        pltpu.make_async_copy(state.at[0], st, sem_in.at[0]),
        pltpu.make_async_copy(mix, mx, sem_in.at[1]),
        pltpu.make_async_copy(skip, sk, sem_in.at[2]),
    ]
    barrier = pltpu.get_barrier_semaphore()

    def greet(off, carry):
        pl.semaphore_signal(barrier, inc=1, device_id=place(lax.rem(n + off, N)), device_id_type=MESH)
        return carry

    lax.fori_loop(1, N, greet, 0)
    own_rows = pltpu.make_async_copy(state.at[0, pl.ds(a * R, R)], ra.at[a], sem_own)
    own_rows.start()
    for load in loads:
        load.start()
    build_forward(ft, K, 32)
    pl.semaphore_wait(barrier, N - 1)

    def row_copy(off, r):
        b = lax.rem(a + off, L)
        return pltpu.make_async_remote_copy(
            src_ref=state.at[0, b * R + r], dst_ref=ra.at[a, r],
            send_sem=sem_a.at[off, r], recv_sem=sem_ra.at[off, r],
            device_id=(b, g), device_id_type=MESH,
        )

    for r in range(R):
        for off in range(1, L):
            row_copy(off, r).start()
    own_rows.wait()
    for r in range(R):
        for off in range(1, L):
            row_copy(off, r).wait_recv()
        rows = ra[:, r].reshape(K, C)
        spectrum = jnp.dot(ft[...], rows, preferred_element_type=F32)
        sb[:, r] = spectrum.reshape(N, 2 * own, C).astype(BF16)

    def spread(stage, src, dst, count, me, target):
        def send(off, carry):
            p = lax.rem(me + off, count)
            pltpu.make_async_remote_copy(
                src_ref=src.at[p], dst_ref=dst.at[me],
                send_sem=sem_s.at[stage], recv_sem=sem_r.at[stage],
                device_id=target(p), device_id_type=MESH,
            ).start()
            return carry

        lax.fori_loop(1, count, send, 0)
        dst[me] = src[me]

    def gathered(stage, dst, count):
        part = dst.at[pl.ds(0, count - 1)]
        pltpu.make_async_copy(part, part, sem_r.at[stage]).wait()

    def drained(stage, src, count):
        part = src.at[pl.ds(0, count - 1)]
        pltpu.make_async_copy(part, part, sem_s.at[stage]).wait()

    spread(0, sb, rb, N, n, place)
    build_legendre(lg, an, syt, n * own)
    gathered(0, rb, N)
    scr[...] = rb[...].astype(F32).reshape(LAT * 2 * own, C)
    for i in range(own):
        pieces = jnp.concatenate(
            [scr[pl.ds(2 * i + part, LAT, stride=2 * own), :] for part in range(2)], axis=1
        ).astype(BF16)
        coeffs = jnp.dot(an[i], pieces, preferred_element_type=F32)
        for part in range(2):
            sc[:, i, part] = coeffs[:, part * C : (part + 1) * C].reshape(G, D, C).astype(BF16)

    def in_plane(h):
        return (a, h)

    spread(1, sc, rc, G, g, in_plane)
    for load in loads:
        load.wait()
    for l in range(D):
        wb[l, :C, :C] = mx[l, 0]
        wb[l, :C, C:] = mx[l, 1]
        wb[l, C:, :C] = -mx[l, 1]
        wb[l, C:, C:] = mx[l, 0]
    build_backward(bt, K, 32)
    gathered(1, rc, G)
    scm[0] = rc[...].astype(F32).reshape(DEG * own * 2, C)
    for l in range(D):
        paired = jnp.concatenate(
            [scm[0, pl.ds(part * D + l, G * own, stride=2 * D), :] for part in range(2)], axis=1
        ).astype(BF16)
        mixed = jnp.dot(paired, wb[l], preferred_element_type=F32)
        for part in range(2):
            scm[1, pl.ds(part * D + l, G * own, stride=2 * D), :] = mixed[:, part * C : (part + 1) * C]
    sd[...] = scm[1].reshape(G, own, 2, D, C).astype(BF16)

    spread(2, sd, rd, G, g, in_plane)
    for j in range(J):
        local[j] = jnp.dot(st[j], sk[...], preferred_element_type=F32)
    gathered(2, rd, G)
    for i in range(own):
        pieces = jnp.concatenate([rd[:, i, part].reshape(DEG, C) for part in range(2)], axis=1)
        gridded = jnp.dot(syt[i], pieces, preferred_element_type=F32)
        for part in range(2):
            scr[pl.ds(2 * i + part, LAT, stride=2 * own), :] = gridded[:, part * C : (part + 1) * C]
    se[...] = scr[...].reshape(N, R, 2 * own, C).astype(BF16)

    spread(3, se, re, N, n, place)
    gathered(3, re, N)

    def sector_copy(off, r):
        b = lax.rem(a + off, L)
        return pltpu.make_async_remote_copy(
            src_ref=sf.at[b, r], dst_ref=rf.at[a, r],
            send_sem=sem_f.at[off, r], recv_sem=sem_rf.at[off, r],
            device_id=(b, g), device_id_type=MESH,
        )

    def inverse(b, r):
        table = bt[pl.ds(pl.multiple_of(b * KD, KD), KD), :]
        modes = re[:, r].reshape(Q, C)
        return jnp.dot(table, modes, preferred_element_type=F32).astype(BF16)

    for r in range(R):
        for off in range(1, L):
            b = lax.rem(a + off, L)
            sf[b, r] = inverse(b, r)
            sector_copy(off, r).start()
    for r in range(R):
        row = a * R + r
        out[0, row] = gelu(inverse(a, r).astype(F32) + local[row]).astype(BF16)
    for r in range(R):
        for off in range(1, L):
            b = lax.rem(a + L - off, L)
            sector_copy(off, r).wait_recv()
            row = b * R + r
            out[0, row] = gelu(rf[b, r].astype(F32) + local[row]).astype(BF16)

    for r in range(R):
        for off in range(1, L):
            row_copy(off, r).wait_send()
            sector_copy(off, r).wait_send()
    drained(0, sb, N)
    drained(1, sc, G)
    drained(2, sd, G)
    drained(3, se, N)


def shards(state, mix_weight, skip_weight):
    samples, J, KD, C = state.shape
    D = mix_weight.shape[0]
    L = lax.axis_size("lon")
    G = lax.axis_size("lat")
    N, R, K, LAT, DEG = L * G, J // L, KD * L, J * G, D * G
    own = K // 2 // N
    Q = 2 * own * N
    wide = (N, R, 2 * own, C)
    deep = (G, own, 2, D, C)
    VMEM = pltpu.VMEM
    DMA = pltpu.SemaphoreType.DMA
    return pl.pallas_call(
        functools.partial(kernel, L, G),
        out_shape=jax.ShapeDtypeStruct(state.shape, BF16),
        in_specs=[pl.BlockSpec(memory_space=pl.ANY)] * 3,
        out_specs=pl.BlockSpec(memory_space=pltpu.VMEM),
        scratch_shapes=[
            VMEM((J, KD, C), BF16),
            VMEM(mix_weight.shape, BF16),
            VMEM((C, C), BF16),
            VMEM((L, R, KD, C), BF16),
            VMEM(wide, BF16), VMEM(wide, BF16),
            VMEM(deep, BF16), VMEM(deep, BF16),
            VMEM(deep, BF16), VMEM(deep, BF16),
            VMEM(wide, BF16), VMEM(wide, BF16),
            VMEM((L, R, KD, C), BF16), VMEM((L, R, KD, C), BF16),
            VMEM((Q, K), BF16), VMEM((K, Q), BF16),
            VMEM((own, DEG, LAT), F32),
            VMEM((own, DEG, LAT), BF16), VMEM((own, LAT, DEG), BF16),
            VMEM((D, 2 * C, 2 * C), BF16),
            VMEM((LAT * 2 * own, C), F32),
            VMEM((2, DEG * own * 2, C), F32),
            VMEM((J, KD, C), F32),
            DMA((3,)), DMA, DMA((L, R)), DMA((L, R)),
            DMA((4,)), DMA((4,)), DMA((L, R)), DMA((L, R)),
        ],
        compiler_params=pltpu.CompilerParams(
            collective_id=0, has_side_effects=True, vmem_limit_bytes=48 * 1024 * 1024
        ),
    )(state, mix_weight, skip_weight)


def solution(mesh):
    placed = (P(None, "lat", "lon", None), P("lat", None, None, None), P())
    return jax.shard_map(
        shards, mesh=mesh, in_specs=placed, out_specs=P(None, "lat", "lon", None), check_vma=False
    )
```

time: 209 us -> 50.8 us (0.24)
  loops' own time: 84.2 us -> 0 us
  Pallas kernels: 0 us -> 47 us
  blocking collectives: 32.9 us -> 0 us
  other arithmetic: 26.6 us -> 0 us
  waiting for transfers between devices: 25.1 us -> 0 us
  starting transfers between devices: 23.4 us -> 0 us
  local copies, waits for them, and re-layouts: 11.8 us -> 3.45 us
  matrix products: 2.38 us -> 0 us
    another operation x1 -> x0, loops' own time: 84.2 us -> none  [legendre_tables(): outputs = lax.scan(advance, (zeros, zeros, zeros), levels, unroll=32)[1]]
    pallas_call x0 -> x1, Pallas kernels: none -> 47 us  [shards(): pl.pallas_call(functools.partial(kernel, L, G), out_shape=jax.ShapeDtypeS...]
    all_to_all x3 -> x0, blocking collectives: 32.9 us -> none  [the longest x1 12.7 us: shards(): lax.all_to_all(mixed, 'lat', split_axis=2, concat_axis=1, tiled=True)]
    all_to_all x5 -> x0, waiting for transfers between devices: 25.1 us -> none  [the longest x1 9.91 us: shards(): lax.all_to_all(coeffs, 'lat', split_axis=1, concat_axis=2, tiled=True)]
    all_to_all x5 -> x0, starting transfers between devices: 23.4 us -> none  [the longest x1 6.19 us: shards(): lax.all_to_all(spectrum, 'lat', split_axis=2, concat_axis=1, tiled=True)]
    while x248 -> x0, other arithmetic: 18 us -> none
    slice x8 -> x0, local copies, waits for them, and re-layouts: 5.69 us -> none  [legendre_tables(): outputs = lax.scan(advance, (zeros, zeros, zeros), levels, unroll=32)[1]]
    sqrt x256 -> x0, other arithmetic: 4.49 us -> none  [the longest x128 2.36 us: advance(): jnp.sqrt(jnp.maximum(4.0 * level * level - 1.0, 0.0) / jnp.maximum(level...]
  transfers between devices with their start and end apart: 5 -> 0, of which waited for: 4 -> 0; matrix products, arithmetic and copies ran while one was open for 16% -> 0% of each run, Pallas kernels for 0% -> 0%
where the time goes in v1:
time: 50.8 us; the launch traced here: 50.5 us
  Pallas kernels  47 us (93%)
  local copies, waits for them, and re-layouts  3.45 us (7%)
    pallas_call x1, Pallas kernels, shards(): pl.pallas_call(functools.partial(kernel, L, G), out_shape=jax.ShapeDtypeS...  47 us
    unnamed x7, local copies, waits for them, and re-layouts  3.45 us

profile of v1, /device:TPU:0, one launch (start us, length us, event | category | flops | bytes accessed | tf_op | source)
XLA Modules:
  0.0 50.5 jit_solution(9943204430472687356)
XLA Ops:
  0.0 0.0 copy-start
  0.0 1.0 %copy-done = bf16[8,2,128,128]{3,2,1,0:T(8,128)(2,1)S(1)} copy-done((bf16[8,2,128,128]{3,2,1,0:T(8,128)(2,1)S(1)}, bf16[8,2,128,128]{3,2,1,0:T(8,128)(2,1)}, u32[]{:S(2)}) %copy-start) | copy-done | bytes 524312
  1.0 0.0 copy-start.1
  1.0 0.9 %copy-done.1 = bf16[1,8,128,128]{3,2,1,0:T(8,128)(2,1)S(1)} copy-done((bf16[1,8,128,128]{3,2,1,0:T(8,128)(2,1)S(1)}, bf16[1,8,128,128]{3,2,1,0:T(8,128)(2,1)}, u32[]{:S(2)}) %copy-start.1) | copy-done | bytes 262168
  2.0 0.0 copy-start.2
  2.0 0.8 %copy-done.2 = bf16[128,128]{1,0:T(8,128)(2,1)S(1)} copy-done((bf16[128,128]{1,0:T(8,128)(2,1)S(1)}, bf16[128,128]{1,0:T(8,128)(2,1)}, u32[]{:S(2)}) %copy-start.2) | copy-done | bytes 32792
  2.8 47.0 %shard_map.37 = bf16[1,8,128,128]{3,2,1,0:T(8,128)(2,1)S(1)} custom-call(bf16[1,8,128,128]{3,2,1,0:T(8,128)(2,1)S(1)} %copy-done.1, bf16[8,2,128,128]{3,2,1,0:T(8,128)(2,1)S(1)} %copy-done, bf16[128,128]{1,0:T(8,128)(2,1)S(1)} %copy-done.2), custom_call_target="tpu_custom_call" | custom-call | tf_op jit(solution)/shard_map/pallas_call | solution.py:290
  49.8 0.7 %copy.5 = bf16[1,8,128,128]{3,2,1,0:T(8,128)(2,1)} copy(bf16[1,8,128,128]{3,2,1,0:T(8,128)(2,1)S(1)} %shard_map.37) | data formatting | bytes 524288
Async XLA Ops:
  0.0 1.0 %copy-start = (bf16[8,2,128,128]{3,2,1,0:T(8,128)(2,1)S(1)}, bf16[8,2,128,128]{3,2,1,0:T(8,128)(2,1)}, u32[]{:S(2)}) copy-start(bf16[8,2,128,128]{3,2,1,0:T(8,128)(2,1)} %mix.1) | copy-start | bytes 1572868
  1.0 0.9 %copy-start.1 = (bf16[1,8,128,128]{3,2,1,0:T(8,128)(2,1)S(1)}, bf16[1,8,128,128]{3,2,1,0:T(8,128)(2,1)}, u32[]{:S(2)}) copy-start(bf16[1,8,128,128]{3,2,1,0:T(8,128)(2,1)} %state.1) | copy-start | bytes 786436
  2.0 0.8 %copy-start.2 = (bf16[128,128]{1,0:T(8,128)(2,1)S(1)}, bf16[128,128]{1,0:T(8,128)(2,1)}, u32[]{:S(2)}) copy-start(bf16[128,128]{1,0:T(8,128)(2,1)} %skip.1) | copy-start | bytes 98308

commit v2 on v1

--- a/solution.py
+++ b/solution.py
@@ -19,36 +19,32 @@
     return value & (size - 1) if size & (size - 1) == 0 else lax.rem(value, size)
 
 
-def fourier_values(mode_index, part, lon_index, lon_count):
-    phase = modulo(lon_index * mode_index + part * (lon_count // 4), lon_count)
-    return jnp.cos(phase.astype(F32) * (2.0 * math.pi / lon_count)) * (1.0 / math.sqrt(lon_count))
-
-
 def build_forward(ft, lon_count, block):
     rows, columns = ft.shape
+    quarter = lon_count // 4
 
     def fill(step, carry):
         start = pl.multiple_of(step * block, block)
         q = lax.broadcasted_iota(jnp.int32, (block, columns), 0) + start
         k = lax.broadcasted_iota(jnp.int32, (block, columns), 1)
-        ft[pl.ds(start, block), :] = fourier_values(q >> 1, q & 1, k, lon_count).astype(BF16)
+        phase = modulo(k * (q >> 1) + (q & 1) * quarter, lon_count)
+        folded = quarter - jnp.minimum(phase, lon_count - phase)
+        angle = folded.astype(F32) * (2.0 * math.pi / lon_count)
+        square = angle * angle
+        total = jnp.full_like(square, 1.0 / math.factorial(13))
+        for power in (11, 9, 7, 5, 3, 1):
+            sign = 1.0 if power % 4 == 1 else -1.0
+            total = total * square + sign / math.factorial(power)
+        ft[pl.ds(start, block), :] = (total * angle * (1.0 / math.sqrt(lon_count))).astype(BF16)
         return carry
 
     lax.fori_loop(0, rows // block, fill, 0)
 
 
-def build_backward(bt, lon_count, block):
-    rows, columns = bt.shape
-
-    def fill(step, carry):
-        start = pl.multiple_of(step * block, block)
-        k = lax.broadcasted_iota(jnp.int32, (block, columns), 0) + start
-        q = lax.broadcasted_iota(jnp.int32, (block, columns), 1)
-        weight = jnp.where(q < 2, 1.0, 2.0)
-        bt[pl.ds(start, block), :] = (fourier_values(q >> 1, q & 1, k, lon_count) * weight).astype(BF16)
-        return carry
-
-    lax.fori_loop(0, rows // block, fill, 0)
+def build_backward(bt, ft, block):
+    rows = ft.shape[0]
+    for start in range(0, rows, block):
+        bt[:, start : start + block] = jnp.transpose(ft[start : start + block, :].astype(F32)).astype(BF16)
 
 
 def build_legendre(lg, an, syt, first_mode):
@@ -100,7 +96,8 @@
     for i in range(own):
         value = lg[i]
         an[i] = (value * (math.pi / math.sqrt(lat_count)) * sine).astype(BF16)
-        syt[i] = jnp.transpose(value * (1.0 / math.sqrt(degrees))).astype(BF16)
+        weight = jnp.where(orders[i : i + 1] == 0.0, 1.0, 2.0)
+        syt[i] = jnp.transpose((value * (1.0 / math.sqrt(degrees))) * weight).astype(BF16)
 
 
 def gelu(v):
@@ -110,8 +107,8 @@
 def kernel(
     L, G, state, mix, skip, out,
     st, mx, sk, ra, sb, rb, sc, rc, sd, rd, se, re, sf, rf,
-    ft, bt, lg, an, syt, wb, scr, scm, local,
-    sem_in, sem_own, sem_a, sem_ra, sem_s, sem_r, sem_f, sem_rf,
+    ft, bt, lg, an, syt, wb, scr, scm, local, ov,
+    sem_out, sem_in, sem_own, sem_a, sem_ra, sem_s, sem_r, sem_f, sem_rf,
 ):
     N = L * G
     J, KD, C = st.shape
@@ -211,7 +208,7 @@
         wb[l, :C, C:] = mx[l, 1]
         wb[l, C:, :C] = -mx[l, 1]
         wb[l, C:, C:] = mx[l, 0]
-    build_backward(bt, K, 32)
+    build_backward(bt, ft, 128)
     gathered(1, rc, G)
     scm[0] = rc[...].astype(F32).reshape(DEG * own * 2, C)
     for l in range(D):
@@ -250,6 +247,10 @@
         modes = re[:, r].reshape(Q, C)
         return jnp.dot(table, modes, preferred_element_type=F32).astype(BF16)
 
+    def result_copy(off, b):
+        rows = pl.ds(b * R, R)
+        return pltpu.make_async_copy(ov.at[rows], out.at[0, rows], sem_out.at[off])
+
     for r in range(R):
         for off in range(1, L):
             b = lax.rem(a + off, L)
@@ -257,18 +258,22 @@
             sector_copy(off, r).start()
     for r in range(R):
         row = a * R + r
-        out[0, row] = gelu(inverse(a, r).astype(F32) + local[row]).astype(BF16)
-    for r in range(R):
-        for off in range(1, L):
-            b = lax.rem(a + L - off, L)
+        ov[row] = gelu(inverse(a, r).astype(F32) + local[row]).astype(BF16)
+    result_copy(0, a).start()
+    for off in range(1, L):
+        b = lax.rem(a + L - off, L)
+        for r in range(R):
             sector_copy(off, r).wait_recv()
             row = b * R + r
-            out[0, row] = gelu(rf[b, r].astype(F32) + local[row]).astype(BF16)
+            ov[row] = gelu(rf[b, r].astype(F32) + local[row]).astype(BF16)
+        result_copy(off, b).start()
 
     for r in range(R):
         for off in range(1, L):
             row_copy(off, r).wait_send()
             sector_copy(off, r).wait_send()
+    for off in range(L):
+        result_copy(off, lax.rem(a + L - off, L)).wait()
     drained(0, sb, N)
     drained(1, sc, G)
     drained(2, sd, G)
@@ -290,8 +295,8 @@
     return pl.pallas_call(
         functools.partial(kernel, L, G),
         out_shape=jax.ShapeDtypeStruct(state.shape, BF16),
-        in_specs=[pl.BlockSpec(memory_space=pl.ANY)] * 3,
-        out_specs=pl.BlockSpec(memory_space=pltpu.VMEM),
+        in_specs=[pl.BlockSpec(memory_space=pltpu.HBM)] * 3,
+        out_specs=pl.BlockSpec(memory_space=pltpu.HBM),
         scratch_shapes=[
             VMEM((J, KD, C), BF16),
             VMEM(mix_weight.shape, BF16),
@@ -308,12 +313,12 @@
             VMEM((D, 2 * C, 2 * C), BF16),
             VMEM((LAT * 2 * own, C), F32),
             VMEM((2, DEG * own * 2, C), F32),
-            VMEM((J, KD, C), F32),
-            DMA((3,)), DMA, DMA((L, R)), DMA((L, R)),
+            VMEM((J, KD, C), F32), VMEM((J, KD, C), BF16),
+            DMA((L,)), DMA((3,)), DMA, DMA((L, R)), DMA((L, R)),
             DMA((4,)), DMA((4,)), DMA((L, R)), DMA((L, R)),
         ],
         compiler_params=pltpu.CompilerParams(
-            collective_id=0, has_side_effects=True, vmem_limit_bytes=48 * 1024 * 1024
+            collective_id=0, has_side_effects=True, vmem_limit_bytes=60 * 1024 * 1024
         ),
     )(state, mix_weight, skip_weight)
 

time: 50.8 us -> 49.6 us (0.976)
  local copies, waits for them, and re-layouts: 3.45 us -> 1.67 us
  Pallas kernels: 47 us -> 47.8 us
    unnamed x7 -> x1, local copies, waits for them, and re-layouts: 3.45 us -> 1.67 us
    pallas_call x1, Pallas kernels: 47 us -> 47.8 us  [shards(): pl.pallas_call(functools.partial(kernel, L, G), out_shape=jax.ShapeDtypeS...]
where the time goes in v2:
time: 49.6 us; the launch traced here: 49.5 us
  Pallas kernels  47.8 us (96%)
  local copies, waits for them, and re-layouts  1.67 us (3%)
    pallas_call x1, Pallas kernels, shards(): pl.pallas_call(functools.partial(kernel, L, G), out_shape=jax.ShapeDtypeS...  47.8 us
    unnamed x1, local copies, waits for them, and re-layouts  1.67 us

profile of v2, /device:TPU:0, one launch (start us, length us, event | category | flops | bytes accessed | tf_op | source)
XLA Modules:
  0.0 49.5 jit_solution(4500054011311067500)
XLA Ops:
  0.0 47.8 %shard_map.37 = bf16[1,8,128,128]{3,2,1,0:T(8,128)(2,1)} custom-call(bf16[1,8,128,128]{3,2,1,0:T(8,128)(2,1)} %state.1, bf16[8,2,128,128]{3,2,1,0:T(8,128)(2,1)} %mix.1, bf16[128,128]{1,0:T(8,128)(2,1)} %skip.1), custom_call_target="tpu_custom_call" | custom-call | tf_op jit(solution)/shard_map/pallas_call | solution.py:295
  47.8 1.7 %copy.5 = bf16[1,8,128,128]{3,2,1,0:T(8,128)(2,1)} copy(bf16[1,8,128,128]{3,2,1,0:T(8,128)(2,1)} %shard_map.37) | data formatting | bytes 524288

commit v3 on v2

--- a/solution.py
+++ b/solution.py
@@ -19,15 +19,17 @@
     return value & (size - 1) if size & (size - 1) == 0 else lax.rem(value, size)
 
 
-def build_forward(ft, lon_count, block):
+def build_forward(ft, lon_count, own, block):
     rows, columns = ft.shape
     quarter = lon_count // 4
+    devices = rows // 2 // own
 
     def fill(step, carry):
         start = pl.multiple_of(step * block, block)
         q = lax.broadcasted_iota(jnp.int32, (block, columns), 0) + start
         k = lax.broadcasted_iota(jnp.int32, (block, columns), 1)
-        phase = modulo(k * (q >> 1) + (q & 1) * quarter, lon_count)
+        mode = modulo(q >> 1, own) * devices + lax.div(q >> 1, own)
+        phase = modulo(k * mode + (q & 1) * quarter, lon_count)
         folded = quarter - jnp.minimum(phase, lon_count - phase)
         angle = folded.astype(F32) * (2.0 * math.pi / lon_count)
         square = angle * angle
@@ -47,16 +49,16 @@
         bt[:, start : start + block] = jnp.transpose(ft[start : start + block, :].astype(F32)).astype(BF16)
 
 
-def build_legendre(lg, an, syt, first_mode):
+def build_legendre(lg, an, syt, first_mode, stride):
     own, degrees, lat_count = lg.shape
     shape = (own, lat_count)
     position = lax.broadcasted_iota(jnp.int32, (1, lat_count), 1).astype(F32)
     colatitude = math.pi * (position + 0.5) / lat_count
     cosine = jnp.cos(colatitude)
     sine = jnp.sin(colatitude)
-    orders = (lax.broadcasted_iota(jnp.int32, shape, 0) + first_mode).astype(F32)
+    orders = (lax.broadcasted_iota(jnp.int32, shape, 0) * stride + first_mode).astype(F32)
     counter = (lax.broadcasted_iota(jnp.int32, (own, degrees), 1) + 1).astype(F32)
-    own_order = (lax.broadcasted_iota(jnp.int32, (own, degrees), 0) + first_mode).astype(F32)
+    own_order = (lax.broadcasted_iota(jnp.int32, (own, degrees), 0) * stride + first_mode).astype(F32)
     halves = 0.5 * jnp.log((2.0 * counter + 1.0) / (2.0 * counter))
     summed = jnp.sum(jnp.where(counter <= own_order, halves, 0.0), axis=1, keepdims=True)
     log_start = 0.5 * math.log(0.5) + summed + orders * jnp.log(sine)
@@ -100,6 +102,10 @@
         syt[i] = jnp.transpose((value * (1.0 / math.sqrt(degrees))) * weight).astype(BF16)
 
 
+def chunk_modes(own):
+    return own // 2 if own % 2 == 0 else own
+
+
 def gelu(v):
     return 0.5 * v * (1.0 + jnp.tanh(math.sqrt(2.0 / math.pi) * (v + 0.044715 * v * v * v)))
 
@@ -109,6 +115,7 @@
     st, mx, sk, ra, sb, rb, sc, rc, sd, rd, se, re, sf, rf,
     ft, bt, lg, an, syt, wb, scr, scm, local, ov,
     sem_out, sem_in, sem_own, sem_a, sem_ra, sem_s, sem_r, sem_f, sem_rf,
+    sem_cs, sem_cr, sem_ds, sem_dr,
 ):
     N = L * G
     J, KD, C = st.shape
@@ -131,6 +138,8 @@
         pltpu.make_async_copy(mix, mx, sem_in.at[1]),
         pltpu.make_async_copy(skip, sk, sem_in.at[2]),
     ]
+    rc[...] = jnp.zeros_like(rc)
+    rd[...] = jnp.zeros_like(rd)
     barrier = pltpu.get_barrier_semaphore()
 
     def greet(off, carry):
@@ -142,7 +151,6 @@
     own_rows.start()
     for load in loads:
         load.start()
-    build_forward(ft, K, 32)
     pl.semaphore_wait(barrier, N - 1)
 
     def row_copy(off, r):
@@ -156,6 +164,7 @@
     for r in range(R):
         for off in range(1, L):
             row_copy(off, r).start()
+    build_forward(ft, K, own, 32)
     own_rows.wait()
     for r in range(R):
         for off in range(1, L):
@@ -185,8 +194,58 @@
         part = src.at[pl.ds(0, count - 1)]
         pltpu.make_async_copy(part, part, sem_s.at[stage]).wait()
 
+    def wanted(i, h, d):
+        return N * i + h * L + a <= D * d + D - 1
+
+    def forth(i, h):
+        return pltpu.make_async_remote_copy(
+            src_ref=sc.at[i, h], dst_ref=rc.at[i, g],
+            send_sem=sem_cs.at[i, h], recv_sem=sem_cr.at[i, g],
+            device_id=(a, h), device_id_type=MESH,
+        )
+
+    def came_forth(i, h):
+        return pltpu.make_async_copy(rc.at[i, h], rc.at[i, h], sem_cr.at[i, h])
+
+    def went_forth(i, h):
+        return pltpu.make_async_copy(sc.at[i, h], sc.at[i, h], sem_cs.at[i, h])
+
+    def back(i, h):
+        return pltpu.make_async_remote_copy(
+            src_ref=sd.at[i, h], dst_ref=rd.at[i, g],
+            send_sem=sem_ds.at[i, h], recv_sem=sem_dr.at[i, g],
+            device_id=(a, h), device_id_type=MESH,
+        )
+
+    def came_back(i, h):
+        return pltpu.make_async_copy(rd.at[i, h], rd.at[i, h], sem_dr.at[i, h])
+
+    def went_back(i, h):
+        return pltpu.make_async_copy(sd.at[i, h], sd.at[i, h], sem_ds.at[i, h])
+
+    def start(copy, i, condition):
+        def act(h):
+            @pl.when(condition(h))
+            def _():
+                copy(i, h).start()
+        return act
+
+    def finish(copy, i, condition):
+        def act(h):
+            @pl.when(condition(h))
+            def _():
+                copy(i, h).wait()
+        return act
+
+    def each_other(act):
+        def step(off, carry):
+            act(lax.rem(g + off, G))
+            return carry
+
+        lax.fori_loop(1, G, step, 0)
+
     spread(0, sb, rb, N, n, place)
-    build_legendre(lg, an, syt, n * own)
+    build_legendre(lg, an, syt, n, N)
     gathered(0, rb, N)
     scr[...] = rb[...].astype(F32).reshape(LAT * 2 * own, C)
     for i in range(own):
@@ -195,12 +254,10 @@
         ).astype(BF16)
         coeffs = jnp.dot(an[i], pieces, preferred_element_type=F32)
         for part in range(2):
-            sc[:, i, part] = coeffs[:, part * C : (part + 1) * C].reshape(G, D, C).astype(BF16)
-
-    def in_plane(h):
-        return (a, h)
-
-    spread(1, sc, rc, G, g, in_plane)
+            sc[i, :, part] = coeffs[:, part * C : (part + 1) * C].reshape(G, D, C).astype(BF16)
+        each_other(start(forth, i, lambda h: wanted(i, g, h)))
+        rc[i, g] = sc[i, g]
+
     for load in loads:
         load.wait()
     for l in range(D):
@@ -208,31 +265,36 @@
         wb[l, :C, C:] = mx[l, 1]
         wb[l, C:, :C] = -mx[l, 1]
         wb[l, C:, C:] = mx[l, 0]
-    build_backward(bt, ft, 128)
-    gathered(1, rc, G)
-    scm[0] = rc[...].astype(F32).reshape(DEG * own * 2, C)
-    for l in range(D):
-        paired = jnp.concatenate(
-            [scm[0, pl.ds(part * D + l, G * own, stride=2 * D), :] for part in range(2)], axis=1
-        ).astype(BF16)
-        mixed = jnp.dot(paired, wb[l], preferred_element_type=F32)
-        for part in range(2):
-            scm[1, pl.ds(part * D + l, G * own, stride=2 * D), :] = mixed[:, part * C : (part + 1) * C]
-    sd[...] = scm[1].reshape(G, own, 2, D, C).astype(BF16)
-
-    spread(2, sd, rd, G, g, in_plane)
+    size = chunk_modes(own)
+    for first in range(0, own, size):
+        for i in range(first, first + size):
+            each_other(finish(came_forth, i, lambda h: wanted(i, h, g)))
+        scm[0] = rc[first : first + size].astype(F32).reshape(size * G * 2 * D, C)
+        for l in range(D):
+            paired = jnp.concatenate(
+                [scm[0, pl.ds(part * D + l, size * G, stride=2 * D), :] for part in range(2)], axis=1
+            ).astype(BF16)
+            mixed = jnp.dot(paired, wb[l], preferred_element_type=F32)
+            for part in range(2):
+                scm[1, pl.ds(part * D + l, size * G, stride=2 * D), :] = mixed[:, part * C : (part + 1) * C]
+        sd[first : first + size] = scm[1].reshape(size, G, 2, D, C).astype(BF16)
+        for i in range(first, first + size):
+            each_other(start(back, i, lambda h: wanted(i, h, g)))
+            rd[i, g] = sd[i, g]
+
     for j in range(J):
         local[j] = jnp.dot(st[j], sk[...], preferred_element_type=F32)
-    gathered(2, rd, G)
+    build_backward(bt, ft, 128)
     for i in range(own):
-        pieces = jnp.concatenate([rd[:, i, part].reshape(DEG, C) for part in range(2)], axis=1)
+        each_other(finish(came_back, i, lambda h: wanted(i, g, h)))
+        pieces = jnp.concatenate([rd[i, :, part].reshape(DEG, C) for part in range(2)], axis=1)
         gridded = jnp.dot(syt[i], pieces, preferred_element_type=F32)
         for part in range(2):
             scr[pl.ds(2 * i + part, LAT, stride=2 * own), :] = gridded[:, part * C : (part + 1) * C]
     se[...] = scr[...].reshape(N, R, 2 * own, C).astype(BF16)
 
-    spread(3, se, re, N, n, place)
-    gathered(3, re, N)
+    spread(1, se, re, N, n, place)
+    gathered(1, re, N)
 
     def sector_copy(off, r):
         b = lax.rem(a + off, L)
@@ -275,9 +337,10 @@
     for off in range(L):
         result_copy(off, lax.rem(a + L - off, L)).wait()
     drained(0, sb, N)
-    drained(1, sc, G)
-    drained(2, sd, G)
-    drained(3, se, N)
+    for i in range(own):
+        each_other(finish(went_forth, i, lambda h: wanted(i, g, h)))
+        each_other(finish(went_back, i, lambda h: wanted(i, h, g)))
+    drained(1, se, N)
 
 
 def shards(state, mix_weight, skip_weight):
@@ -289,14 +352,14 @@
     own = K // 2 // N
     Q = 2 * own * N
     wide = (N, R, 2 * own, C)
-    deep = (G, own, 2, D, C)
+    deep = (own, G, 2, D, C)
     VMEM = pltpu.VMEM
     DMA = pltpu.SemaphoreType.DMA
     return pl.pallas_call(
         functools.partial(kernel, L, G),
         out_shape=jax.ShapeDtypeStruct(state.shape, BF16),
         in_specs=[pl.BlockSpec(memory_space=pltpu.HBM)] * 3,
-        out_specs=pl.BlockSpec(memory_space=pltpu.HBM),
+        out_specs=pl.BlockSpec(memory_space=pltpu.VMEM),
         scratch_shapes=[
             VMEM((J, KD, C), BF16),
             VMEM(mix_weight.shape, BF16),
@@ -312,10 +375,11 @@
             VMEM((own, DEG, LAT), BF16), VMEM((own, LAT, DEG), BF16),
             VMEM((D, 2 * C, 2 * C), BF16),
             VMEM((LAT * 2 * own, C), F32),
-            VMEM((2, DEG * own * 2, C), F32),
+            VMEM((2, DEG * chunk_modes(own) * 2, C), F32),
             VMEM((J, KD, C), F32), VMEM((J, KD, C), BF16),
             DMA((L,)), DMA((3,)), DMA, DMA((L, R)), DMA((L, R)),
-            DMA((4,)), DMA((4,)), DMA((L, R)), DMA((L, R)),
+            DMA((2,)), DMA((2,)), DMA((L, R)), DMA((L, R)),
+            DMA((own, G)), DMA((own, G)), DMA((own, G)), DMA((own, G)),
         ],
         compiler_params=pltpu.CompilerParams(
             collective_id=0, has_side_effects=True, vmem_limit_bytes=60 * 1024 * 1024

time: 49.6 us -> 50.2 us (1.012)
  no operation moved by 1% of the time
where the time goes in v3:
time: 50.2 us; the launch traced here: 49.9 us
  Pallas kernels  48.2 us (96%)
  local copies, waits for them, and re-layouts  1.67 us (3%)
    pallas_call x1, Pallas kernels, shards(): pl.pallas_call(functools.partial(kernel, L, G), out_shape=jax.ShapeDtypeS...  48.2 us
    unnamed x1, local copies, waits for them, and re-layouts  1.67 us

profile of v3, /device:TPU:0, one launch (start us, length us, event | category | flops | bytes accessed | tf_op | source)
XLA Modules:
  0.0 49.9 jit_solution(5676378431552928192)
XLA Ops:
  0.0 48.2 %shard_map.37 = bf16[1,8,128,128]{3,2,1,0:T(8,128)(2,1)} custom-call(bf16[1,8,128,128]{3,2,1,0:T(8,128)(2,1)} %state.1, bf16[8,2,128,128]{3,2,1,0:T(8,128)(2,1)} %mix.1, bf16[128,128]{1,0:T(8,128)(2,1)} %skip.1), custom_call_target="tpu_custom_call" | custom-call | tf_op jit(solution)/shard_map/pallas_call | solution.py:358
  48.2 1.7 %copy.5 = bf16[1,8,128,128]{3,2,1,0:T(8,128)(2,1)} copy(bf16[1,8,128,128]{3,2,1,0:T(8,128)(2,1)} %shard_map.37) | data formatting | bytes 524288

commit v4 on v3

--- a/solution.py
+++ b/solution.py
@@ -13,6 +13,18 @@
 log_rescale = 18.0 * math.log(10.0)
 F32 = jnp.float32
 BF16 = jnp.bfloat16
+
+
+def repeat(first, last, body):
+    if last - first > 64:
+        lax.fori_loop(first, last, body, 0)
+    else:
+        for index in range(first, last):
+            body(index, 0)
+
+
+def ring(value, count):
+    return jnp.where(value >= count, value - count, value)
 
 
 def modulo(value, size):
@@ -143,15 +155,40 @@
     barrier = pltpu.get_barrier_semaphore()
 
     def greet(off, carry):
-        pl.semaphore_signal(barrier, inc=1, device_id=place(lax.rem(n + off, N)), device_id_type=MESH)
+        pl.semaphore_signal(barrier, inc=1, device_id=place(ring(n + off, N)), device_id_type=MESH)
         return carry
 
-    lax.fori_loop(1, N, greet, 0)
+    repeat(1, N, greet)
     own_rows = pltpu.make_async_copy(state.at[0, pl.ds(a * R, R)], ra.at[a], sem_own)
     own_rows.start()
     for load in loads:
         load.start()
     pl.semaphore_wait(barrier, N - 1)
+
+    def halves(split):
+        step = R // 2 if split and R % 2 == 0 else R
+        return [(s, pl.ds(s * step, step)) for s in range(R // step)]
+
+    def spread(stage, src, dst, count, me, target, rows):
+        def send(off, carry):
+            p = ring(me + off, count)
+            pltpu.make_async_remote_copy(
+                src_ref=src.at[p, rows], dst_ref=dst.at[me, rows],
+                send_sem=sem_s.at[stage], recv_sem=sem_r.at[stage],
+                device_id=target(p), device_id_type=MESH,
+            ).start()
+            return carry
+
+        repeat(1, count, send)
+        dst[me, rows] = src[me, rows]
+
+    def gathered(stage, dst, count, rows):
+        part = dst.at[pl.ds(0, count - 1), rows]
+        pltpu.make_async_copy(part, part, sem_r.at[stage]).wait()
+
+    def drained(stage, src, count, rows):
+        part = src.at[pl.ds(0, count - 1), rows]
+        pltpu.make_async_copy(part, part, sem_s.at[stage]).wait()
 
     def row_copy(off, r):
         b = lax.rem(a + off, L)
@@ -172,27 +209,9 @@
         rows = ra[:, r].reshape(K, C)
         spectrum = jnp.dot(ft[...], rows, preferred_element_type=F32)
         sb[:, r] = spectrum.reshape(N, 2 * own, C).astype(BF16)
-
-    def spread(stage, src, dst, count, me, target):
-        def send(off, carry):
-            p = lax.rem(me + off, count)
-            pltpu.make_async_remote_copy(
-                src_ref=src.at[p], dst_ref=dst.at[me],
-                send_sem=sem_s.at[stage], recv_sem=sem_r.at[stage],
-                device_id=target(p), device_id_type=MESH,
-            ).start()
-            return carry
-
-        lax.fori_loop(1, count, send, 0)
-        dst[me] = src[me]
-
-    def gathered(stage, dst, count):
-        part = dst.at[pl.ds(0, count - 1)]
-        pltpu.make_async_copy(part, part, sem_r.at[stage]).wait()
-
-    def drained(stage, src, count):
-        part = src.at[pl.ds(0, count - 1)]
-        pltpu.make_async_copy(part, part, sem_s.at[stage]).wait()
+        for s, part_rows in halves(True):
+            if r == part_rows.start + part_rows.size - 1:
+                spread(s, sb, rb, N, n, place, part_rows)
 
     def wanted(i, h, d):
         return N * i + h * L + a <= D * d + D - 1
@@ -239,14 +258,14 @@
 
     def each_other(act):
         def step(off, carry):
-            act(lax.rem(g + off, G))
+            act(ring(g + off, G))
             return carry
 
-        lax.fori_loop(1, G, step, 0)
-
-    spread(0, sb, rb, N, n, place)
+        repeat(1, G, step)
+
     build_legendre(lg, an, syt, n, N)
-    gathered(0, rb, N)
+    for s, part_rows in halves(True):
+        gathered(s, rb, N, part_rows)
     scr[...] = rb[...].astype(F32).reshape(LAT * 2 * own, C)
     for i in range(own):
         pieces = jnp.concatenate(
@@ -293,8 +312,8 @@
             scr[pl.ds(2 * i + part, LAT, stride=2 * own), :] = gridded[:, part * C : (part + 1) * C]
     se[...] = scr[...].reshape(N, R, 2 * own, C).astype(BF16)
 
-    spread(1, se, re, N, n, place)
-    gathered(1, re, N)
+    for s, part_rows in halves(True):
+        spread(2 + s, se, re, N, n, place, part_rows)
 
     def sector_copy(off, r):
         b = lax.rem(a + off, L)
@@ -314,6 +333,9 @@
         return pltpu.make_async_copy(ov.at[rows], out.at[0, rows], sem_out.at[off])
 
     for r in range(R):
+        for s, part_rows in halves(True):
+            if r == part_rows.start:
+                gathered(2 + s, re, N, part_rows)
         for off in range(1, L):
             b = lax.rem(a + off, L)
             sf[b, r] = inverse(b, r)
@@ -336,11 +358,13 @@
             sector_copy(off, r).wait_send()
     for off in range(L):
         result_copy(off, lax.rem(a + L - off, L)).wait()
-    drained(0, sb, N)
+    for s, part_rows in halves(True):
+        drained(s, sb, N, part_rows)
     for i in range(own):
         each_other(finish(went_forth, i, lambda h: wanted(i, g, h)))
         each_other(finish(went_back, i, lambda h: wanted(i, h, g)))
-    drained(1, se, N)
+    for s, part_rows in halves(True):
+        drained(2 + s, se, N, part_rows)
 
 
 def shards(state, mix_weight, skip_weight):
@@ -378,7 +402,7 @@
             VMEM((2, DEG * chunk_modes(own) * 2, C), F32),
             VMEM((J, KD, C), F32), VMEM((J, KD, C), BF16),
             DMA((L,)), DMA((3,)), DMA, DMA((L, R)), DMA((L, R)),
-            DMA((2,)), DMA((2,)), DMA((L, R)), DMA((L, R)),
+            DMA((4,)), DMA((4,)), DMA((L, R)), DMA((L, R)),
             DMA((own, G)), DMA((own, G)), DMA((own, G)), DMA((own, G)),
         ],
         compiler_params=pltpu.CompilerParams(

time: 50.2 us -> 47.9 us (0.954)
  Pallas kernels: 48.2 us -> 46.1 us
    pallas_call x1, Pallas kernels: 48.2 us -> 46.1 us  [shards(): pl.pallas_call(functools.partial(kernel, L, G), out_shape=jax.ShapeDtypeS...]
where the time goes in v4:
time: 47.9 us; the launch traced here: 47.7 us
  Pallas kernels  46.1 us (96%)
  local copies, waits for them, and re-layouts  1.67 us (3%)
    pallas_call x1, Pallas kernels, shards(): pl.pallas_call(functools.partial(kernel, L, G), out_shape=jax.ShapeDtypeS...  46.1 us
    unnamed x1, local copies, waits for them, and re-layouts  1.67 us

profile of v4, /device:TPU:0, one launch (start us, length us, event | category | flops | bytes accessed | tf_op | source)
XLA Modules:
  0.0 47.7 jit_solution(7621009503854560806)
XLA Ops:
  0.0 46.1 %shard_map.37 = bf16[1,8,128,128]{3,2,1,0:T(8,128)(2,1)} custom-call(bf16[1,8,128,128]{3,2,1,0:T(8,128)(2,1)} %state.1, bf16[8,2,128,128]{3,2,1,0:T(8,128)(2,1)} %mix.1, bf16[128,128]{1,0:T(8,128)(2,1)} %skip.1), custom_call_target="tpu_custom_call" | custom-call | tf_op jit(solution)/shard_map/pallas_call | solution.py:382
  46.1 1.7 %copy.5 = bf16[1,8,128,128]{3,2,1,0:T(8,128)(2,1)} copy(bf16[1,8,128,128]{3,2,1,0:T(8,128)(2,1)} %shard_map.37) | data formatting | bytes 524288
